TPU v7x, 256 devices: a whole 4x4x8 slice. The times are simulated.
256 devices in a mesh: section: 4 (over x), tp: 16 (over y, z_hi, core), dp: 4 (over z_lo).
Axes of the slice: x: 4, y: 4, z: 8 (z_hi: 2, z_lo: 4; z = z_hi * 4 + z_lo), core: 2. Of those that a mesh axis runs over, the one named last changes fastest.
Arguments:
- responses: bfloat16 [2048, 8192], P(('section', 'tp'), 'dp'), may hold values from -6 to 6
- weights: bfloat16 [4, 8192, 16384], P('section', 'dp', 'tp'), may hold values from -0.0625 to 0.0625
- readout: float32 [4, 16384], P('section', 'tp'), may hold values from -0.09375 to 0.09375
- lengths: int32 [16], replicated, may hold values from 1 to 256, 2048 in all
- groups: int32 [16], replicated, may hold values from 0 to 3
Outputs:
- weight_grad: bfloat16 [4, 2048, 16384], P('dp', 'section', 'tp')
- policy_loss: float32 [], replicated
Inputs may be any that keep to these rules, and one draw needn't show every extreme that they name: The lengths add up to 2048; the longest response has exactly 256 tokens.
All inputs are finite; a program needn't handle non-finite values.
Results may differ from a plain program's by a relative error of at most 0.005.
Values may be sent and summed in bfloat16 or wider, within the bound.
A program may use at most 64 MiB of HBM per device.

v0:
```python
import jax
import jax.numpy as jnp
from jax import lax
from jax.sharding import PartitionSpec as P

kl_weight = 0.2


def from_root(block, axis, source):
    block = jnp.where(lax.axis_index(axis) == source, block, jnp.zeros_like(block))
    return lax.psum(block, axis)


def advantages(rewards, groups):
    same_group = (groups[:, None] == groups[None, :]).astype(jnp.float32)
    members = jnp.sum(same_group, axis=1)
    group_mean = jnp.sum(same_group * rewards[None, :], axis=1) / members
    spread = jnp.sum(same_group * (rewards[None, :] - group_mean[:, None]) ** 2, axis=1) / members
    return (rewards - group_mean) / jnp.sqrt(spread + 1.0)


def contract_rows(left, right):
    return lax.dot_general(
        left, right, (((0,), (0,)), ((), ())), preferred_element_type=jnp.float32
    )


def local(responses, weights, readout, lengths, groups):
    gathered = lax.all_gather(responses, ("section", "tp"), axis=0, tiled=True)
    weight_block = weights[0]
    total_rows = gathered.shape[0]
    row_block = total_rows // lax.axis_size("dp")
    hidden = lax.psum_scatter(
        jnp.dot(gathered, weight_block, preferred_element_type=jnp.float32),
        "dp",
        scatter_dimension=0,
        tiled=True,
    )
    read_row = readout[0]
    partial_score = jnp.sum(jax.nn.silu(hidden) * read_row[None, :], axis=1)
    own_score = lax.psum(partial_score, "tp")
    joined = lax.all_gather(own_score[None, :], "section", axis=0, tiled=True)
    resp_count = lengths.shape[0]
    first_row = lax.axis_index("dp") * row_block
    position = first_row + jnp.arange(row_block, dtype=jnp.int32)
    starts = jnp.cumsum(lengths) - lengths
    finish = starts + lengths
    in_response = (
        (position[:, None] >= starts[None, :]) & (position[:, None] < finish[None, :])
    ).astype(jnp.float32)
    last_token = (position[:, None] == finish[None, :] - 1).astype(jnp.float32)
    token_len = jnp.sum(in_response * lengths.astype(jnp.float32)[None, :], axis=1)
    lp_old = jax.nn.log_sigmoid(joined[0])
    lp_ref = jax.nn.log_sigmoid(joined[1])
    lp_new = jax.nn.log_sigmoid(joined[3])
    prob_ratio = jnp.exp(lp_new - lp_old)
    log_gap = lp_ref - lp_new
    penalty = kl_weight * (jnp.exp(log_gap) - log_gap - 1.0)
    reward_part = jnp.sum(last_token * joined[2][:, None], axis=0)
    rewards = lax.psum(reward_part, "dp")
    advantage = advantages(rewards, groups)
    token_adv = jnp.sum(in_response * advantage[None, :], axis=1)
    token_loss = -prob_ratio * token_adv + penalty
    policy_loss = lax.psum(jnp.sum(token_loss / token_len), "dp") / resp_count
    coeff = (
        total_rows
        / (resp_count * token_len)
        * (-prob_ratio * token_adv + kl_weight * (1.0 - jnp.exp(log_gap)))
        * jax.nn.sigmoid(-joined[3])
    )
    sigmoid_z = jax.nn.sigmoid(hidden)
    silu_slope = sigmoid_z * (1.0 + hidden * (1.0 - sigmoid_z))
    hidden_grad = (coeff[:, None] * read_row[None, :] * silu_slope).astype(jnp.bfloat16)
    block_width = gathered.shape[1] // lax.axis_size("section")
    feature_block = lax.dynamic_slice_in_dim(
        gathered, lax.axis_index("section") * block_width, block_width, 1
    )
    learner_index = lax.axis_size("section") - 1
    all_grad = lax.all_gather(hidden_grad, "dp", axis=0, tiled=True)
    shared_grad = from_root(all_grad, "section", learner_index)
    weight_grad = contract_rows(feature_block, shared_grad)
    return (weight_grad.astype(jnp.bfloat16)[None], policy_loss)


def solution(mesh):
    return jax.shard_map(
        local,
        mesh=mesh,
        in_specs=(
            P(("section", "tp"), "dp"),
            P("section", "dp", "tp"),
            P("section", "tp"),
            P(),
            P(),
        ),
        out_specs=(P("dp", "section", "tp"), P()),
        check_vma=False,
    )
```

profile of v0, /device:TPU:1, one launch (start us, length us, event | category | flops | bytes accessed | tf_op | source)
XLA Modules:
  0.0 557.4 jit_solution(10904170529704305852)
XLA Ops:
  7.2 0.0 all-gather.4.cloned.1.call-start
  7.2 0.7 all-gather.4.cloned.1.call-update
  7.9 0.0 reduce-scatter.2.cloned.1.call-start
  7.9 120.6 %all-gather.4.cloned.1.call-done = bf16[2048,2048]{1,0:T(8,128)(2,1)} async-done(((bf16[32,2048]{1,0:T(8,128)(2,1)}), bf16[2048,2048]{1,0:T(8,128)(2,1)}) %all-gather.4.cloned.1.call-update) | async-done | bytes 8388624 | tf_op jit(solution)/shard_map/all_gather | solution.py:29
  128.5 14.4 %fusion = f32[2048,1024]{1,0:T(8,128)} fusion(bf16[2048,2048]{1,0:T(8,128)(2,1)} %all-gather.4.cloned.1.call-done, bf16[1,2048,1024]{2,1,0:T(8,128)(2,1)} %param.6), kind=kOutput, calls=%fused_computation | convolution fusion | flops 8589934592 | bytes 20971520 | tf_op jit(solution)/shard_map/dot_general | solution.py:34
  143.0 0.0 reduce-scatter.2.cloned.1.call-update
  143.0 0.0 copy-start.2
  143.0 0.0 all-gather.6.cloned.1.call-start
  143.1 0.6 copy-done.3
  143.6 0.1 copy.10
  143.7 0.1 reduce
  143.9 142.4 %reduce-scatter.2.cloned.1.call-done = f32[512,1024]{1,0:T(8,128)} async-done(((f32[2048,1024]{1,0:T(8,128)}), f32[512,1024]{1,0:T(8,128)}) %reduce-scatter.2.cloned.1.call-update) | async-done | bytes 2097168 | tf_op jit(solution)/shard_map/reduce_scatter | solution.py:33
  286.2 0.0 copy-done.1
  286.2 2.4 multiply_reduce_fusion
  288.6 43.0 %psum.28 = f32[1,512]{1,0:T(1,128)S(1)} all-reduce(f32[1,512]{1,0:T(1,128)S(1)} %bitcast.22), channel_id=1, replica_groups=mesh['section'=4,'tp'=16,'dp'=4] {'tp'}, use_global_device_ids=true, to_apply=%region_4.5 | all-reduce | flops 512 | bytes 4096 | tf_op jit(solution)/shard_map/psum | solution.py:41
  331.6 8.9 %all-gather = f32[4,1,512]{2,1,0:T(1,128)S(1)} all-gather(f32[1,1,512]{2,1,0:T(1,128)S(1)} %bitcast.25), channel_id=1, replica_groups=mesh['section'=4,'tp'=16,'dp'=4] {'section'}, dimensions={0}, use_global_device_ids=true | all-gather | bytes 10240 | tf_op jit(solution)/shard_map/all_gather | solution.py:42
  340.5 0.2 select_reduce_fusion.1
  340.7 9.4 %psum.29 = f32[16]{0:T(128)S(1)} all-reduce(f32[16]{0:T(128)S(1)} %select_reduce_fusion.1), channel_id=1, replica_groups=mesh['section'=4,'tp'=16,'dp'=4] {'dp'}, use_global_device_ids=true, to_apply=%region_6.7 | all-reduce | flops 16 | bytes 128 | tf_op jit(solution)/shard_map/psum | solution.py:60
  350.1 0.0 copy-done.2
  350.1 0.2 fusion.11
  350.3 0.2 fusion.12
  350.5 0.1 select_reduce_fusion.2
  350.6 0.6 fusion.28
  351.3 1.8 multiply_convert_fusion
  353.1 0.0 all-gather.6.cloned.1.call-update
  353.1 0.0 all-reduce.2.cloned.1.call-start
  353.1 88.0 %all-gather.6.cloned.1.call-done = bf16[2048,1024]{1,0:T(8,128)(2,1)} async-done(((bf16[512,1024]{1,0:T(8,128)(2,1)}), bf16[2048,1024]{1,0:T(8,128)(2,1)}) %all-gather.6.cloned.1.call-update) | async-done | bytes 4194320 | tf_op jit(solution)/shard_map/all_gather | solution.py:79
  441.2 2.2 broadcast_select_fusion
  443.4 0.0 all-reduce.2.cloned.1.call-update
  443.4 8.6 %psum.31 = f32[]{:T(128)} all-reduce(f32[]{:T(128)} %get-tuple-element.6), channel_id=1, replica_groups=mesh['section'=4,'tp'=16,'dp'=4] {'dp'}, use_global_device_ids=true, to_apply=%region_13.14 | all-reduce | flops 1 | bytes 8 | tf_op jit(solution)/shard_map/psum | solution.py:64
  452.7 90.9 %all-reduce.2.cloned.1.call-done = bf16[2048,1024]{1,0:T(8,128)(2,1)} async-done(((bf16[2048,1024]{1,0:T(8,128)(2,1)}), bf16[2048,1024]{1,0:T(8,128)(2,1)}) %all-reduce.2.cloned.1.call-update) | async-done | bytes 4194320 | tf_op jit(solution)/shard_map/psum | solution.py:11
  543.6 6.2 %fusion.7 = bf16[1,512,1024]{2,1,0:T(8,128)(2,1)} fusion(bf16[2048,1024]{1,0:T(8,128)(2,1)} %all-reduce.2.cloned.1.call-done, bf16[2048,2048]{1,0:T(8,128)(2,1)} %all-gather.4.cloned.1.call-done, s32[]{:T(128)S(6)} %select_n.34), kind=kOutput, calls=%fused_computation.9 | convolution fusion | flops 2148007936 | bytes 7340036 | tf_op jit(solution)/shard_map/dot_general | solution.py:23
  (11 shorter events, 0.1 us)
Async XLA Ops:
  7.2 121.4 %all-gather.4.cloned.1.call-start = ((), (), s32[]{:S(2)}) async-start(), calls=%async_computation.1 | async-start | bytes 8519680 | tf_op jit(solution)/shard_map/all_gather | solution.py:29
  7.9 278.3 %reduce-scatter.2.cloned.1.call-start = ((), (), s32[]{:S(2)}) async-start(), calls=%async_computation.2 | async-start | bytes 10485760 | tf_op jit(solution)/shard_map/reduce_scatter | solution.py:33
  143.0 0.7 copy-start.3
  143.0 143.3 %copy-start.1 = (f32[1,1024]{1,0:T(1,128)S(1)}, f32[1,1024]{1,0:T(1,128)}, u32[]{:S(2)}) copy-start(f32[1,1024]{1,0:T(1,128)} %param.7) | copy-start | bytes 12292
  143.0 207.1 %copy-start.2 = (s32[16]{0:T(128)S(1)}, s32[16]{0:T(128)}, u32[]{:S(2)}) copy-start(s32[16]{0:T(128)} %param.9) | copy-start | bytes 196
  143.0 298.2 %all-gather.6.cloned.1.call-start = ((), (), s32[]{:S(2)}) async-start(), calls=%async_computation.3 | async-start | bytes 5242880 | tf_op jit(solution)/shard_map/all_gather | solution.py:79
  286.2 65.0 %copy-start = (f32[512,1024]{1,0:T(8,128)S(1)}, f32[512,1024]{1,0:T(8,128)}, u32[]{:S(2)}) copy-start(f32[512,1024]{1,0:T(8,128)} %reduce-scatter.2.cloned.1.call-done) | copy-start | bytes 6291460
  353.1 190.5 %all-reduce.2.cloned.1.call-start = ((), (), s32[]{:S(2)}) async-start(), calls=%async_computation.4 | async-start | bytes 8388608 | tf_op jit(solution)/shard_map/psum | solution.py:11
Sparse Core Ops, SparseCore 0:
  11.5 117.0 all-gather.3
  143.1 143.0 reduce-scatter.1
  353.2 87.9 all-gather.5
  443.6 99.9 all-reduce.1
where the time goes:
time: 558 us; the launch traced here: 557 us
  waiting for transfers between devices  443 us (79%)
  blocking collectives  69.9 us (13%)
  matrix products  20.6 us (4%)
  between operations  15.6 us (3%)
  other arithmetic  7.89 us (1%)
    reduce_scatter x1, waiting for transfers between devices, local(): lax.psum_scatter(jnp.dot(gathered, weight_block, preferred_element_type=j...  142 us
    all_gather x1, waiting for transfers between devices, local(): gathered = lax.all_gather(responses, ('section', 'tp'), axis=0, tiled=True)  121 us
    psum x1, waiting for transfers between devices, from_root(): return lax.psum(block, axis)  90.9 us
    all_gather x1, waiting for transfers between devices, local(): all_grad = lax.all_gather(hidden_grad, 'dp', axis=0, tiled=True)  88 us
    psum x1, blocking collectives, local(): own_score = lax.psum(partial_score, 'tp')  43 us
    dot_general x1, matrix products, local(): jnp.dot(gathered, weight_block, preferred_element_type=jnp.float32)  14.4 us
  transfers between devices with their start and end apart: 4, of which 4 were waited for; matrix products, arithmetic and copies ran while one was open for 0% of the time, Pallas kernels for 0%

commit v1 on v0

--- a/solution.py
+++ b/solution.py
@@ -6,9 +6,14 @@
 kl_weight = 0.2
 
 
+def entries_mix(slab_in, dev_axis):
+    y2 = lax.all_gather(slab_in, dev_axis).sum(axis=0)
+    return y2
+
+
 def from_root(block, axis, source):
     block = jnp.where(lax.axis_index(axis) == source, block, jnp.zeros_like(block))
-    return lax.psum(block, axis)
+    return entries_mix(block, axis)
 
 
 def advantages(rewards, groups):

time: 558 us -> 629 us (1.13)
  waiting for transfers between devices: 443 us -> 501 us
  other arithmetic: 7.89 us -> 20 us
    all_gather x0 -> x1, waiting for transfers between devices: none -> 150 us  [entries_mix(): y2 = lax.all_gather(slab_in, dev_axis).sum(axis=0)]
    psum x1 -> x0, waiting for transfers between devices: 90.9 us -> none  [from_root(): return lax.psum(block, axis)]
    reduce_sum x0 -> x1, other arithmetic: none -> 12.1 us  [entries_mix(): y2 = lax.all_gather(slab_in, dev_axis).sum(axis=0)]
where the time goes in v1:
time: 629 us; the launch traced here: 628 us
  waiting for transfers between devices  501 us (80%)
  blocking collectives  69.8 us (11%)
  matrix products  20.6 us (3%)
  other arithmetic  20 us (3%)
  between operations  15.6 us (2%)
    all_gather x1, waiting for transfers between devices, entries_mix(): y2 = lax.all_gather(slab_in, dev_axis).sum(axis=0)  150 us
    reduce_scatter x1, waiting for transfers between devices, local(): lax.psum_scatter(jnp.dot(gathered, weight_block, preferred_element_type=j...  142 us
    all_gather x1, waiting for transfers between devices, local(): gathered = lax.all_gather(responses, ('section', 'tp'), axis=0, tiled=True)  121 us
    all_gather x1, waiting for transfers between devices, local(): all_grad = lax.all_gather(hidden_grad, 'dp', axis=0, tiled=True)  88 us
    psum x1, blocking collectives, local(): own_score = lax.psum(partial_score, 'tp')  42.9 us
    dot_general x1, matrix products, local(): jnp.dot(gathered, weight_block, preferred_element_type=jnp.float32)  14.4 us
  transfers between devices with their start and end apart: 4, of which 4 were waited for; matrix products, arithmetic and copies ran while one was open for 0% of the time, Pallas kernels for 0%

profile of v1, /device:TPU:1, one launch (start us, length us, event | category | flops | bytes accessed | tf_op | source)
XLA Modules:
  0.0 628.3 jit_solution(10447645399820581998)
XLA Ops:
  7.2 0.0 all-gather.6.cloned.1.call-start
  7.2 0.7 all-gather.6.cloned.1.call-update
  7.9 0.0 reduce-scatter.2.cloned.1.call-start
  7.9 120.6 %all-gather.6.cloned.1.call-done = bf16[2048,2048]{1,0:T(8,128)(2,1)} async-done(((bf16[32,2048]{1,0:T(8,128)(2,1)}), bf16[2048,2048]{1,0:T(8,128)(2,1)}) %all-gather.6.cloned.1.call-update) | async-done | bytes 8388624 | tf_op jit(solution)/shard_map/all_gather | solution.py:34
  128.6 14.4 %fusion = f32[2048,1024]{1,0:T(8,128)} fusion(bf16[2048,2048]{1,0:T(8,128)(2,1)} %all-gather.6.cloned.1.call-done, bf16[1,2048,1024]{2,1,0:T(8,128)(2,1)} %param.6), kind=kOutput, calls=%fused_computation | convolution fusion | flops 8589934592 | bytes 20971520 | tf_op jit(solution)/shard_map/dot_general | solution.py:39
  143.0 0.0 reduce-scatter.2.cloned.1.call-update
  143.0 0.0 copy-start.2
  143.0 0.0 all-gather.8.cloned.1.call-start
  143.1 0.6 copy-done.3
  143.7 0.1 copy.10
  143.8 0.1 reduce.1
  143.9 142.4 %reduce-scatter.2.cloned.1.call-done = f32[512,1024]{1,0:T(8,128)} async-done(((f32[2048,1024]{1,0:T(8,128)}), f32[512,1024]{1,0:T(8,128)}) %reduce-scatter.2.cloned.1.call-update) | async-done | bytes 2097168 | tf_op jit(solution)/shard_map/reduce_scatter | solution.py:38
  286.3 0.0 copy-done.1
  286.3 2.4 multiply_reduce_fusion
  288.7 42.9 %psum.21 = f32[1,512]{1,0:T(1,128)S(1)} all-reduce(f32[1,512]{1,0:T(1,128)S(1)} %bitcast.24), channel_id=1, replica_groups=mesh['section'=4,'tp'=16,'dp'=4] {'tp'}, use_global_device_ids=true, to_apply=%region_4.5 | all-reduce | flops 512 | bytes 4096 | tf_op jit(solution)/shard_map/psum | solution.py:46
  331.6 8.9 %all-gather.1 = f32[4,1,512]{2,1,0:T(1,128)S(1)} all-gather(f32[1,1,512]{2,1,0:T(1,128)S(1)} %bitcast.27), channel_id=1, replica_groups=mesh['section'=4,'tp'=16,'dp'=4] {'section'}, dimensions={0}, use_global_device_ids=true | all-gather | bytes 10240 | tf_op jit(solution)/shard_map/all_gather | solution.py:47
  340.5 0.2 select_reduce_fusion.1
  340.7 9.4 %psum.22 = f32[16]{0:T(128)S(1)} all-reduce(f32[16]{0:T(128)S(1)} %select_reduce_fusion.1), channel_id=1, replica_groups=mesh['section'=4,'tp'=16,'dp'=4] {'dp'}, use_global_device_ids=true, to_apply=%region_6.7 | all-reduce | flops 16 | bytes 128 | tf_op jit(solution)/shard_map/psum | solution.py:65
  350.2 0.2 fusion.11
  350.4 0.2 fusion.12
  350.6 0.1 select_reduce_fusion.2
  350.7 0.6 fusion.28
  351.3 1.8 multiply_convert_fusion
  353.1 0.0 all-gather.8.cloned.1.call-update
  353.1 0.0 all-gather.10.cloned.1.call-start
  353.2 88.0 %all-gather.8.cloned.1.call-done = bf16[2048,1024]{1,0:T(8,128)(2,1)} async-done(((bf16[512,1024]{1,0:T(8,128)(2,1)}), bf16[2048,1024]{1,0:T(8,128)(2,1)}) %all-gather.8.cloned.1.call-update) | async-done | bytes 4194320 | tf_op jit(solution)/shard_map/all_gather | solution.py:84
  441.2 2.3 broadcast_select_fusion
  443.5 0.0 all-gather.10.cloned.1.call-update
  443.5 8.6 %psum.23 = f32[]{:T(128)} all-reduce(f32[]{:T(128)} %get-tuple-element.6), channel_id=1, replica_groups=mesh['section'=4,'tp'=16,'dp'=4] {'dp'}, use_global_device_ids=true, to_apply=%region_13.14 | all-reduce | flops 1 | bytes 8 | tf_op jit(solution)/shard_map/psum | solution.py:69
  452.7 149.7 %all-gather.10.cloned.1.call-done = bf16[8192,1024]{1,0:T(8,128)(2,1)} async-done(((bf16[2048,1024]{1,0:T(8,128)(2,1)}), bf16[8192,1024]{1,0:T(8,128)(2,1)}) %all-gather.10.cloned.1.call-update) | async-done | bytes 16777232 | tf_op jit(solution)/shard_map/all_gather | solution.py:10
  602.4 12.1 %reduce_sum.91 = bf16[2048,1024]{1,0:T(8,128)(2,1)} reduce(bf16[4,2048,1024]{2,1,0:T(8,128)(2,1)} %bitcast.17, bf16[]{:T(256)} %constant.51.clone.1), dimensions={0}, to_apply=%region_11.12 | reduce | flops 6291456 | bytes 20971522 | tf_op jit(solution)/shard_map/reduce_sum | solution.py:10
  614.5 6.2 fusion.7
  (12 shorter events, 0.1 us)
Async XLA Ops:
  7.2 121.4 %all-gather.6.cloned.1.call-start = ((), (), s32[]{:S(2)}) async-start(), calls=%async_computation.1 | async-start | bytes 8519680 | tf_op jit(solution)/shard_map/all_gather | solution.py:34
  7.9 278.4 %reduce-scatter.2.cloned.1.call-start = ((), (), s32[]{:S(2)}) async-start(), calls=%async_computation.2 | async-start | bytes 10485760 | tf_op jit(solution)/shard_map/reduce_scatter | solution.py:38
  143.0 0.7 copy-start.3
  143.0 143.3 %copy-start.1 = (f32[1,1024]{1,0:T(1,128)S(1)}, f32[1,1024]{1,0:T(1,128)}, u32[]{:S(2)}) copy-start(f32[1,1024]{1,0:T(1,128)} %param.7) | copy-start | bytes 12292
  143.0 207.1 %copy-start.2 = (s32[16]{0:T(128)S(1)}, s32[16]{0:T(128)}, u32[]{:S(2)}) copy-start(s32[16]{0:T(128)} %param.9) | copy-start | bytes 196
  143.0 298.2 %all-gather.8.cloned.1.call-start = ((), (), s32[]{:S(2)}) async-start(), calls=%async_computation.3 | async-start | bytes 5242880 | tf_op jit(solution)/shard_map/all_gather | solution.py:84
  286.3 65.0 %copy-start = (f32[512,1024]{1,0:T(8,128)S(1)}, f32[512,1024]{1,0:T(8,128)}, u32[]{:S(2)}) copy-start(f32[512,1024]{1,0:T(8,128)} %reduce-scatter.2.cloned.1.call-done) | copy-start | bytes 6291460
  353.1 249.3 %all-gather.10.cloned.1.call-start = ((), (), s32[]{:S(2)}) async-start(), calls=%async_computation.4 | async-start | bytes 20971520 | tf_op jit(solution)/shard_map/all_gather | solution.py:10
Sparse Core Ops, SparseCore 0:
  11.5 117.0 all-gather.5
  143.1 143.1 reduce-scatter.1
  353.2 87.9 all-gather.7
  443.6 158.7 all-gather.9
